TPU v7x, 256 devices: a whole 4x4x8 slice. The times are simulated.
256 devices in a mesh: rep: 2 (over core), exp: 128 (over x, y, z).
Axes of the slice: x: 4, y: 4, z: 8, core: 2. Of those that a mesh axis runs over, the one named last changes fastest.
Arguments:
- attn_out: bfloat16 [16384, 4096], P(('rep', 'exp')), may hold values from -6 to 6
- out_weight: bfloat16 [4096, 2048], P('exp'), may hold values from -0.09375 to 0.09375
- router_weight: bfloat16 [2048, 128], replicated, may hold values from -0.125 to 0.125
- gate_weight: bfloat16 [128, 2048, 768], P('exp'), may hold values from -0.125 to 0.125
- up_weight: bfloat16 [128, 2048, 768], P('exp'), may hold values from -0.125 to 0.125
- down_weight: bfloat16 [128, 768, 2048], P('exp'), may hold values from -0.21875 to 0.21875
- cotangent: bfloat16 [16384, 2048], P(('rep', 'exp')), may hold values from -6 to 6
- log_ratios: float32 [16384], P(('rep', 'exp')), may hold values from -0.03 to 0.05
- expert_ids: int32 [16384, 8], P(('rep', 'exp')), may hold values from 0 to 127, as said below
- slot_ids: int32 [16384, 8], P(('rep', 'exp')), may hold values from 0 to 5, as said below
- episode_ids: int32 [16384], P(('rep', 'exp')), may hold values from 0 to 255, never falling along the last dimension, each value on 1 to 256 neighbouring positions
Outputs:
- token_grads: bfloat16 [16384, 4096], P(('rep', 'exp'))
- router_grad: float32 [2048, 128], P('exp')
Inputs may be any that keep to these rules, and one draw needn't show every extreme that they name: `expert_ids`: each row names 8 different experts. Among the rows of one device no expert is named more than 6 times, and on every device some expert is named exactly 6 times. `slot_ids`: among the rows of one device, the pairs of a row with one expert named in it get distinct slots; the slots of one expert on one device are 0 up to the number of its pairs there minus 1. `episode_ids`: episodes are runs of consecutive tokens, numbered in order; each has 1 to 256 tokens, one exactly 256.
All inputs are finite; a program needn't handle non-finite values.
Results may differ from a plain program's by a relative error of at most 0.012.
Values may be sent and summed in bfloat16 or wider, within the bound.
No kernel may reach another device: no remote copies, remote signals or barrier semaphores. Data moves between devices by JAX's collectives and lax.ppermute only.
A program may use at most 128 MiB of HBM per device.

v0:
```python
import jax
import jax.numpy as jnp
from jax import lax
from jax.sharding import PartitionSpec as P

clip_top = 4.0


def shards(
    attn_out,
    out_weight,
    router_weight,
    gate_weight,
    up_weight,
    down_weight,
    cotangent,
    log_ratios,
    expert_ids,
    slot_ids,
    episode_ids,
):
    tok_count = attn_out.shape[0]
    top_count = expert_ids.shape[1]
    model_width = cotangent.shape[1]
    expert_count = lax.axis_size("exp")
    device_count = lax.axis_size("rep") * expert_count
    capacity = 3 * tok_count * top_count // (2 * expert_count)
    episode_count = tok_count * device_count // 64
    episode_hits = (
        episode_ids[:, None] == jnp.arange(episode_count, dtype=jnp.int32)[None, :]
    ).astype(jnp.float32)
    part_logs = jnp.sum(episode_hits * log_ratios[:, None], axis=0)
    part_counts = jnp.sum(episode_hits, axis=0)
    log_sums, counts = lax.psum((part_logs, part_counts), ("rep", "exp"))
    episode_weight = jnp.minimum(jnp.exp(log_sums), clip_top)
    mean_weight = jnp.sum(counts * episode_weight) / (tok_count * device_count)
    token_scale = jnp.sum(episode_hits * episode_weight[None, :], axis=1) / mean_weight
    weight_full = lax.all_gather(out_weight, "exp", axis=0, tiled=True)
    hidden = jnp.dot(attn_out, weight_full, preferred_element_type=jnp.float32).astype(jnp.bfloat16)
    logits = jnp.dot(hidden, router_weight, preferred_element_type=jnp.float32)
    expert_hits = (expert_ids[:, :, None] == jnp.arange(expert_count, dtype=jnp.int32)).astype(
        jnp.float32
    )
    chosen = jnp.sum(expert_hits * logits[:, None, :], axis=2)
    raised = jnp.exp(chosen)
    gate_probs = raised / jnp.sum(raised, axis=1, keepdims=True)
    targets = expert_ids * capacity + slot_ids
    slot_count = expert_count * capacity
    labels = jnp.arange(tok_count, dtype=jnp.int32)[:, None] + 1
    matches = (targets[:, :, None] == jnp.arange(slot_count, dtype=jnp.int32)).astype(jnp.int32)
    owners = jnp.sum(matches * labels[:, :, None], axis=(0, 1))
    filled = owners > 0
    source_rows = jnp.maximum(owners - 1, 0)
    zero_value = jnp.zeros((), jnp.bfloat16)
    send_hidden = jnp.where(filled[:, None], hidden[source_rows], zero_value).reshape(
        expert_count, capacity, model_width
    )
    send_cot = jnp.where(filled[:, None], cotangent[source_rows], zero_value).reshape(
        expert_count, capacity, model_width
    )
    rows_in = lax.all_to_all(send_hidden, "exp", split_axis=0, concat_axis=0, tiled=True)
    cot_in = lax.all_to_all(send_cot, "exp", split_axis=0, concat_axis=0, tiled=True)
    gate_pre = jnp.einsum(
        "snd,df->snf", rows_in, gate_weight[0], preferred_element_type=jnp.float32
    )
    up_pre = jnp.einsum("snd,df->snf", rows_in, up_weight[0], preferred_element_type=jnp.float32)
    upstream = jnp.einsum("snd,fd->snf", cot_in, down_weight[0], preferred_element_type=jnp.float32)
    sigmoid_gate = jax.nn.sigmoid(gate_pre)
    slot_score = jnp.sum(upstream * (gate_pre * sigmoid_gate * up_pre), axis=2)
    grad_gate = (upstream * up_pre * sigmoid_gate * (1.0 + gate_pre * (1.0 - sigmoid_gate))).astype(
        jnp.bfloat16
    )
    grad_up = (upstream * gate_pre * sigmoid_gate).astype(jnp.bfloat16)
    back_rows = (
        jnp.einsum("snf,df->snd", grad_gate, gate_weight[0], preferred_element_type=jnp.float32)
        + jnp.einsum("snf,df->snd", grad_up, up_weight[0], preferred_element_type=jnp.float32)
    ).astype(jnp.bfloat16)
    back_home = lax.all_to_all(back_rows, "exp", split_axis=0, concat_axis=0, tiled=True)
    score_home = lax.all_to_all(slot_score, "exp", split_axis=0, concat_axis=0, tiled=True)
    pair_back = back_home.reshape(slot_count, model_width)[targets]
    pair_score = score_home.reshape(slot_count)[targets]
    mixed_back = jnp.sum(gate_probs[:, :, None] * pair_back.astype(jnp.float32), axis=1)
    logit_grad = gate_probs * (pair_score - jnp.sum(gate_probs * pair_score, axis=1, keepdims=True))
    full_grad = jnp.sum(expert_hits * logit_grad[:, :, None], axis=1)
    weighted = (token_scale[:, None] * full_grad).astype(jnp.bfloat16)
    router_part = jnp.einsum("td,te->de", hidden, weighted, preferred_element_type=jnp.float32)
    grad_hidden = (
        token_scale[:, None] * mixed_back
        + jnp.dot(weighted, router_weight.T, preferred_element_type=jnp.float32)
    ).astype(jnp.bfloat16)
    token_grads = jnp.dot(grad_hidden, weight_full.T, preferred_element_type=jnp.float32).astype(
        jnp.bfloat16
    )
    router_total = lax.psum(router_part, ("rep", "exp"))
    row_count = model_width // expert_count
    router_grad = lax.dynamic_slice_in_dim(
        router_total, lax.axis_index("exp") * row_count, row_count, 0
    )
    return (token_grads, router_grad)


def solution(mesh):
    placed = (
        P(("rep", "exp"), None),
        P("exp", None),
        P(),
        P("exp", None, None),
        P("exp", None, None),
        P("exp", None, None),
        P(("rep", "exp"), None),
        P(("rep", "exp")),
        P(("rep", "exp"), None),
        P(("rep", "exp"), None),
        P(("rep", "exp")),
    )
    return jax.shard_map(
        shards,
        mesh=mesh,
        in_specs=placed,
        out_specs=(P(("rep", "exp"), None), P("exp", None)),
        check_vma=False,
    )
```

profile of v0, /device:TPU:2, one launch (start us, length us, event | category | flops | bytes accessed | tf_op | source)
XLA Modules:
  0.0 948.8 jit_solution(6600559267684554942)
XLA Ops:
  7.2 0.7 all-gather.2.cloned.1.call-update
  7.9 0.8 compare_select_fusion
  8.7 0.1 copy.31
  8.8 0.2 select_reduce_fusion
  9.1 0.2 gt.11
  9.3 4.3 gather_fusion
  13.5 6.3 gather.17
  19.8 144.6 %all-gather.2.cloned.1.call-done = bf16[4096,2048]{1,0:T(8,128)(2,1)} async-done(((bf16[32,2048]{1,0:T(8,128)(2,1)}), bf16[4096,2048]{1,0:T(8,128)(2,1)}) %all-gather.2.cloned.1.call-update) | async-done | bytes 16777232 | tf_op jit(solution)/shard_map/all_gather | solution.py:38
  164.4 9.0 convolution_convert_fusion.1
  173.4 4.3 gather_fusion.1
  177.7 6.2 gather.19
  184.0 5.2 broadcast_select_fusion.1
  189.2 106.0 %all_to_all.24 = bf16[128,6,2048]{2,1,0:T(8,128)(2,1)} all-to-all(bf16[128,6,2048]{2,1,0:T(8,128)(2,1)S(1)} %get-tuple-element.9), channel_id=1, replica_groups=mesh['rep'=2,'exp'=128] {'exp'}, dimensions={0} | all-to-all | bytes 6291456 | tf_op jit(solution)/shard_map/all_to_all | solution.py:61
  295.2 10.3 %all-to-all-start = ((bf16[128,6,2048]{2,1,0:T(8,128)(2,1)}), bf16[128,6,2048]{2,1,0:T(8,128)(2,1)}, u32[]{:S(2)}, u32[]{:S(2)}) async-start(bf16[128,6,2048]{2,1,0:T(8,128)(2,1)} %get-tuple-element.8), calls=%async_computation | async-start | bytes 8388608 | tf_op jit(solution)/shard_map/all_to_all | solution.py:62
  305.6 9.3 fusion.3
  314.9 7.5 fusion.6
  322.4 76.0 %all-to-all-done = bf16[128,6,2048]{2,1,0:T(8,128)(2,1)} async-done(((bf16[128,6,2048]{2,1,0:T(8,128)(2,1)}), bf16[128,6,2048]{2,1,0:T(8,128)(2,1)}, u32[]{:S(2)}, u32[]{:S(2)}) %all-to-all-start) | async-done | bytes 3145760 | tf_op jit(solution)/shard_map/all_to_all | solution.py:62
  398.5 11.8 %multiply_reduce_fusion = (f32[128,6]{0,1:T(8,128)S(1)}, f32[128,6,768]{2,0,1:T(8,128)}) fusion(f32[128,6,768]{2,0,1:T(8,128)} %fusion.6, f32[128,6,768]{2,0,1:T(8,128)} %fusion.3, bf16[1,768,2048]{2,1,0:T(8,128)(2,1)} %param.16, bf16[128,6,2048]{2,1,0:T(8,128)(2,1)} %all-to-all-done), kind=kOutput, calls=%fused_computation.20 | convolution fusion | flops 2420047104 | bytes 13372416 | tf_op jit(solution)/shard_map/snd,fd->snf/dot_general | solution.py:67
  410.3 0.7 copy.37
  411.1 8.7 all-to-all-start.3
  419.8 5.6 fusion.1
  425.4 2.9 add_convert_fusion
  428.3 3.7 copy.35
  432.1 14.4 %all-to-all-start.2 = ((bf16[128,6,2048]{2,1,0:T(8,128)(2,1)}), bf16[128,6,2048]{2,1,0:T(8,128)(2,1)}, u32[]{:S(2)}, u32[]{:S(2)}) async-start(bf16[128,6,2048]{2,1,0:T(8,128)(2,1)} %copy.35), calls=%async_computation.2 | async-start | bytes 8388608 | tf_op jit(solution)/shard_map/all_to_all | solution.py:78
  446.5 0.1 copy.30
  446.6 0.1 copy.36
  446.7 0.1 reshape.135
  446.8 0.1 select_reduce_fusion.4
  446.9 130.2 %psum.21 = f32[256]{0:T(256)S(1)} all-reduce(f32[256]{0:T(256)S(1)} %select_reduce_fusion.4), channel_id=1, replica_groups=mesh['rep'=2,'exp'=128] {'rep','exp'}, use_global_device_ids=true, to_apply=%region_1.0 | all-reduce | flops 256 | bytes 2048 | tf_op jit(solution)/shard_map/psum | solution.py:34
  577.1 0.2 convert_reduce_fusion
  577.3 74.9 %psum.22 = f32[256]{0:T(256)S(1)} all-reduce(f32[256]{0:T(256)S(1)} %get-tuple-element.2), channel_id=1, replica_groups=mesh['rep'=2,'exp'=128] {'rep','exp'}, use_global_device_ids=true, to_apply=%region_4.0 | all-reduce | flops 256 | bytes 2048 | tf_op jit(solution)/shard_map/psum | solution.py:34
  652.2 0.6 multiply_reduce_fusion.2
  653.5 0.2 fusion.21
  653.7 0.2 select_reduce_fusion.2
  653.9 0.1 exponential_reduce_fusion
  654.1 0.5 broadcast.151
  654.6 0.8 reduce.3
  655.4 0.1 reshape.116
  655.5 2.3 gather_fusion.3
  657.9 0.2 multiply_reduce_fusion.1
  658.2 0.2 select_reduce_fusion.1
  658.4 1.3 fusion.20
  659.8 255.7 %all-reduce.2.cloned.1.call-done = f32[2048,128]{1,0:T(8,128)} async-done(((f32[2048,128]{1,0:T(8,128)}), f32[2048,128]{1,0:T(8,128)}) %all-reduce.2.cloned.1.call-update) | async-done | bytes 1048592 | tf_op jit(solution)/shard_map/psum | solution.py:94
  915.5 1.3 constant_dynamic-slice_fusion
  916.8 4.9 reshape.115
  921.7 3.3 gather_fusion.2
  925.0 4.2 fusion
  929.2 12.5 %convolution_convert_fusion = bf16[64,4096]{1,0:T(8,128)(2,1)} fusion(bf16[4096,2048]{1,0:T(8,128)(2,1)} %all-gather.2.cloned.1.call-done, bf16[2048,128]{1,0:T(8,128)(2,1)} %param.13, f32[64,2048]{1,0:T(8,128)} %fusion, f32[64]{0:T(128)S(1)} %broadcast_divide_fusion, f32[64,128]{1,0:T(8,128)S(1)} %select_reduce_fusion.1), kind=kOutput, calls=%fused_computation.5 | convolution fusion | flops 1107968000 | bytes 18383104 | tf_op jit(solution)/shard_map/dot_general | solution.py:91
  (38 shorter events, 0.4 us)
Async XLA Ops:
  7.2 298.4 %copy-start = (bf16[1,2048,768]{2,1,0:T(8,128)(2,1)S(1)}, bf16[1,2048,768]{2,1,0:T(8,128)(2,1)}, u32[]{:S(2)}) copy-start(bf16[1,2048,768]{2,1,0:T(8,128)(2,1)} %param.14) | copy-start | bytes 9437188
  7.2 2.1 copy-start.2
  7.2 157.2 %all-gather.2.cloned.1.call-start = ((), (), s32[]{:S(2)}) async-start(), calls=%async_computation.4 | async-start | bytes 16908288 | tf_op jit(solution)/shard_map/all_gather | solution.py:38
  295.2 103.3 %all-to-all-start = ((bf16[128,6,2048]{2,1,0:T(8,128)(2,1)}), bf16[128,6,2048]{2,1,0:T(8,128)(2,1)}, u32[]{:S(2)}, u32[]{:S(2)}) async-start(bf16[128,6,2048]{2,1,0:T(8,128)(2,1)} %get-tuple-element.8), calls=%async_computation | async-start | bytes 8388608 | tf_op jit(solution)/shard_map/all_to_all | solution.py:62
  305.5 9.4 copy-start.3
  305.5 9.4 copy-start.8
  411.1 21.0 %all-to-all-start.3 = ((f32[128,1,6]{2,1,0:T(1,128)}), f32[128,1,6]{2,1,0:T(1,128)S(1)}, u32[]{:S(2)}, u32[]{:S(2)}) async-start(f32[128,1,6]{2,1,0:T(1,128)} %copy.37), calls=%async_computation.3 | async-start | bytes 131072 | tf_op jit(solution)/shard_map/all_to_all | solution.py:79
  419.8 5.6 copy-start.9
  419.8 5.6 copy-start.10
  419.8 5.6 copy-start.11
  432.0 14.5 %copy-start.5 = (s32[64,8]{0,1:T(8,128)S(1)}, s32[64,8]{0,1:T(8,128)}, u32[]{:S(2)}) copy-start(s32[64,8]{0,1:T(8,128)} %param.19) | copy-start | bytes 6148
  432.0 14.8 %copy-start.6 = (s32[64]{0:T(128)S(1)}, s32[64]{0:T(128)}, u32[]{:S(2)}) copy-start(s32[64]{0:T(128)} %param.21) | copy-start | bytes 772
  432.0 14.8 %copy-start.7 = (f32[64]{0:T(128)S(1)}, f32[64]{0:T(128)}, u32[]{:S(2)}) copy-start(f32[64]{0:T(128)} %param.18) | copy-start | bytes 772
  432.1 221.4 %copy-start.4 = (bf16[2048,128]{1,0:T(8,128)(2,1)S(1)}, bf16[2048,128]{1,0:T(8,128)(2,1)}, u32[]{:S(2)}) copy-start(bf16[2048,128]{1,0:T(8,128)(2,1)} %param.13) | copy-start | bytes 1572868
  432.1 484.7 %all-to-all-start.2 = ((bf16[128,6,2048]{2,1,0:T(8,128)(2,1)}), bf16[128,6,2048]{2,1,0:T(8,128)(2,1)}, u32[]{:S(2)}, u32[]{:S(2)}) async-start(bf16[128,6,2048]{2,1,0:T(8,128)(2,1)} %copy.35), calls=%async_computation.2 | async-start | bytes 8388608 | tf_op jit(solution)/shard_map/all_to_all | solution.py:78
  446.5 469.0 %all-reduce.2.cloned.1.call-start = ((), (), s32[]{:S(2)}) async-start(), calls=%async_computation.5 | async-start | bytes 2097152 | tf_op jit(solution)/shard_map/psum | solution.py:94
  929.2 12.5 %copy-start.1 = (bf16[1,2048,768]{2,1,0:T(8,128)(2,1)S(1)}, bf16[1,2048,768]{2,1,0:T(8,128)(2,1)}, u32[]{:S(2)}) copy-start(bf16[1,2048,768]{2,1,0:T(8,128)(2,1)} %param.14) | copy-start | bytes 9437188
Sparse Core Ops, SparseCore 0:
  11.6 152.7 all-gather.1
  659.9 255.5 all-reduce.1
where the time goes:
time: 957 us; the launch traced here: 949 us
  waiting for transfers between devices  477 us (50%)
  blocking collectives  311 us (32%)
  matrix products  60.2 us (6%)
  local copies, waits for them, and re-layouts  38.7 us (4%)
  starting transfers between devices  33.5 us (4%)
  between operations  15.2 us (2%)
  other arithmetic  13 us (1%)
    psum x1, waiting for transfers between devices, shards(): router_total = lax.psum(router_part, ('rep', 'exp'))  256 us
    psum x2, blocking collectives, shards(): log_sums, counts = lax.psum((part_logs, part_counts), ('rep', 'exp'))  205 us
    all_gather x1, waiting for transfers between devices, shards(): weight_full = lax.all_gather(out_weight, 'exp', axis=0, tiled=True)  145 us
    all_to_all x1, blocking collectives, shards(): lax.all_to_all(send_hidden, 'exp', split_axis=0, concat_axis=0, tiled=True)  106 us
    all_to_all x1, waiting for transfers between devices, shards(): lax.all_to_all(send_cot, 'exp', split_axis=0, concat_axis=0, tiled=True)  76 us
  transfers between devices with their start and end apart: 5, of which 3 were waited for; matrix products, arithmetic and copies ran while one was open for 5% of the time, Pallas kernels for 0%

commit v1 on v0

--- a/solution.py
+++ b/solution.py
@@ -91,7 +91,8 @@
     token_grads = jnp.dot(grad_hidden, weight_full.T, preferred_element_type=jnp.float32).astype(
         jnp.bfloat16
     )
-    router_total = lax.psum(router_part, ("rep", "exp"))
+    half = lax.psum(router_part, "exp")
+    router_total = lax.psum(half, "rep")
     row_count = model_width // expert_count
     router_grad = lax.dynamic_slice_in_dim(
         router_total, lax.axis_index("exp") * row_count, row_count, 0

time: 957 us -> 952 us (level)
    psum x1 -> x2, waiting for transfers between devices: 256 us -> 250 us  [the longest x1 220 us: shards(): half = lax.psum(router_part, 'exp')]
  transfers between devices with their start and end apart: 5 -> 6, of which waited for: 3 -> 4; matrix products, arithmetic and copies ran while one was open for 5% -> 5% of each run, Pallas kernels for 0% -> 0%
where the time goes in v1:
time: 952 us; the launch traced here: 943 us
  waiting for transfers between devices  472 us (50%)
  blocking collectives  311 us (33%)
  matrix products  60.2 us (6%)
  local copies, waits for them, and re-layouts  38.7 us (4%)
  starting transfers between devices  33.5 us (4%)
  between operations  14.9 us (2%)
  other arithmetic  13 us (1%)
    psum x1, waiting for transfers between devices, shards(): half = lax.psum(router_part, 'exp')  220 us
    psum x2, blocking collectives, shards(): log_sums, counts = lax.psum((part_logs, part_counts), ('rep', 'exp'))  205 us
    all_gather x1, waiting for transfers between devices, shards(): weight_full = lax.all_gather(out_weight, 'exp', axis=0, tiled=True)  145 us
    all_to_all x1, blocking collectives, shards(): lax.all_to_all(send_hidden, 'exp', split_axis=0, concat_axis=0, tiled=True)  106 us
    all_to_all x1, waiting for transfers between devices, shards(): lax.all_to_all(send_cot, 'exp', split_axis=0, concat_axis=0, tiled=True)  76 us
    psum x1, waiting for transfers between devices, shards(): router_total = lax.psum(half, 'rep')  30.2 us
  transfers between devices with their start and end apart: 6, of which 4 were waited for; matrix products, arithmetic and copies ran while one was open for 5% of the time, Pallas kernels for 0%

profile of v1, /device:TPU:2, one launch (start us, length us, event | category | flops | bytes accessed | tf_op | source)
XLA Modules:
  0.0 943.1 jit_solution(17831124089875176316)
XLA Ops:
  7.2 0.7 all-gather.2.cloned.1.call-update
  7.9 0.8 compare_select_fusion
  8.7 0.1 copy.31
  8.8 0.2 select_reduce_fusion
  9.1 0.2 gt.11
  9.3 4.3 gather_fusion
  13.5 6.3 gather.17
  19.8 144.6 %all-gather.2.cloned.1.call-done = bf16[4096,2048]{1,0:T(8,128)(2,1)} async-done(((bf16[32,2048]{1,0:T(8,128)(2,1)}), bf16[4096,2048]{1,0:T(8,128)(2,1)}) %all-gather.2.cloned.1.call-update) | async-done | bytes 16777232 | tf_op jit(solution)/shard_map/all_gather | solution.py:38
  164.4 9.0 convolution_convert_fusion.1
  173.4 4.3 gather_fusion.1
  177.7 6.2 gather.19
  184.0 5.2 broadcast_select_fusion.1
  189.2 106.0 %all_to_all.24 = bf16[128,6,2048]{2,1,0:T(8,128)(2,1)} all-to-all(bf16[128,6,2048]{2,1,0:T(8,128)(2,1)S(1)} %get-tuple-element.9), channel_id=1, replica_groups=mesh['rep'=2,'exp'=128] {'exp'}, dimensions={0} | all-to-all | bytes 6291456 | tf_op jit(solution)/shard_map/all_to_all | solution.py:61
  295.2 10.3 %all-to-all-start = ((bf16[128,6,2048]{2,1,0:T(8,128)(2,1)}), bf16[128,6,2048]{2,1,0:T(8,128)(2,1)}, u32[]{:S(2)}, u32[]{:S(2)}) async-start(bf16[128,6,2048]{2,1,0:T(8,128)(2,1)} %get-tuple-element.8), calls=%async_computation | async-start | bytes 8388608 | tf_op jit(solution)/shard_map/all_to_all | solution.py:62
  305.6 9.3 fusion.3
  314.9 7.5 fusion.6
  322.4 76.0 %all-to-all-done = bf16[128,6,2048]{2,1,0:T(8,128)(2,1)} async-done(((bf16[128,6,2048]{2,1,0:T(8,128)(2,1)}), bf16[128,6,2048]{2,1,0:T(8,128)(2,1)}, u32[]{:S(2)}, u32[]{:S(2)}) %all-to-all-start) | async-done | bytes 3145760 | tf_op jit(solution)/shard_map/all_to_all | solution.py:62
  398.5 11.8 %multiply_reduce_fusion = (f32[128,6]{0,1:T(8,128)S(1)}, f32[128,6,768]{2,0,1:T(8,128)}) fusion(f32[128,6,768]{2,0,1:T(8,128)} %fusion.6, f32[128,6,768]{2,0,1:T(8,128)} %fusion.3, bf16[1,768,2048]{2,1,0:T(8,128)(2,1)} %param.16, bf16[128,6,2048]{2,1,0:T(8,128)(2,1)} %all-to-all-done), kind=kOutput, calls=%fused_computation.20 | convolution fusion | flops 2420047104 | bytes 13372416 | tf_op jit(solution)/shard_map/snd,fd->snf/dot_general | solution.py:67
  410.3 0.7 copy.37
  411.1 8.7 all-to-all-start.3
  419.8 5.6 fusion.1
  425.4 2.9 add_convert_fusion
  428.3 3.7 copy.35
  432.1 14.4 %all-to-all-start.2 = ((bf16[128,6,2048]{2,1,0:T(8,128)(2,1)}), bf16[128,6,2048]{2,1,0:T(8,128)(2,1)}, u32[]{:S(2)}, u32[]{:S(2)}) async-start(bf16[128,6,2048]{2,1,0:T(8,128)(2,1)} %copy.35), calls=%async_computation.2 | async-start | bytes 8388608 | tf_op jit(solution)/shard_map/all_to_all | solution.py:78
  446.5 0.1 copy.30
  446.7 0.1 reshape.135
  446.8 0.1 select_reduce_fusion.4
  446.9 130.2 %psum.28 = f32[256]{0:T(256)S(1)} all-reduce(f32[256]{0:T(256)S(1)} %select_reduce_fusion.4), channel_id=1, replica_groups=mesh['rep'=2,'exp'=128] {'rep','exp'}, use_global_device_ids=true, to_apply=%region_1.0 | all-reduce | flops 256 | bytes 2048 | tf_op jit(solution)/shard_map/psum | solution.py:34
  577.1 0.2 convert_reduce_fusion
  577.3 74.9 %psum.29 = f32[256]{0:T(256)S(1)} all-reduce(f32[256]{0:T(256)S(1)} %get-tuple-element.2), channel_id=1, replica_groups=mesh['rep'=2,'exp'=128] {'rep','exp'}, use_global_device_ids=true, to_apply=%region_4.0 | all-reduce | flops 256 | bytes 2048 | tf_op jit(solution)/shard_map/psum | solution.py:34
  652.2 0.6 multiply_reduce_fusion.2
  653.5 0.2 fusion.21
  653.7 0.2 select_reduce_fusion.2
  653.9 0.1 exponential_reduce_fusion
  654.0 0.5 broadcast.151
  654.6 0.8 reduce.3
  655.4 0.1 reshape.116
  655.5 2.3 gather_fusion.3
  657.9 0.2 multiply_reduce_fusion.1
  658.2 0.2 select_reduce_fusion.1
  658.4 1.3 fusion.20
  659.8 220.1 %all-reduce.3.cloned.1.call-done = f32[2048,128]{1,0:T(8,128)} async-done(((f32[2048,128]{1,0:T(8,128)}), f32[2048,128]{1,0:T(8,128)}) %all-reduce.3.cloned.1.call-update) | async-done | bytes 1048592 | tf_op jit(solution)/shard_map/psum | solution.py:94
  879.9 30.2 %all-reduce.5.cloned.1.call-done = f32[2048,128]{1,0:T(8,128)} async-done(((f32[2048,128]{1,0:T(8,128)}), f32[2048,128]{1,0:T(8,128)}) %all-reduce.5.cloned.1.call-update) | async-done | bytes 1048592 | tf_op jit(solution)/shard_map/psum | solution.py:95
  910.1 1.3 constant_dynamic-slice_fusion
  911.4 4.9 reshape.115
  916.3 3.3 gather_fusion.2
  919.6 4.2 fusion
  923.9 12.5 %convolution_convert_fusion = bf16[64,4096]{1,0:T(8,128)(2,1)} fusion(bf16[4096,2048]{1,0:T(8,128)(2,1)} %all-gather.2.cloned.1.call-done, bf16[2048,128]{1,0:T(8,128)(2,1)} %param.13, f32[64,2048]{1,0:T(8,128)} %fusion, f32[64]{0:T(128)S(1)} %broadcast_divide_fusion, f32[64,128]{1,0:T(8,128)S(1)} %select_reduce_fusion.1), kind=kOutput, calls=%fused_computation.5 | convolution fusion | flops 1107968000 | bytes 18383104 | tf_op jit(solution)/shard_map/dot_general | solution.py:91
  (41 shorter events, 0.5 us)
Async XLA Ops:
  7.2 298.4 %copy-start = (bf16[1,2048,768]{2,1,0:T(8,128)(2,1)S(1)}, bf16[1,2048,768]{2,1,0:T(8,128)(2,1)}, u32[]{:S(2)}) copy-start(bf16[1,2048,768]{2,1,0:T(8,128)(2,1)} %param.14) | copy-start | bytes 9437188
  7.2 2.1 copy-start.2
  7.2 157.2 %all-gather.2.cloned.1.call-start = ((), (), s32[]{:S(2)}) async-start(), calls=%async_computation.4 | async-start | bytes 16908288 | tf_op jit(solution)/shard_map/all_gather | solution.py:38
  295.2 103.3 %all-to-all-start = ((bf16[128,6,2048]{2,1,0:T(8,128)(2,1)}), bf16[128,6,2048]{2,1,0:T(8,128)(2,1)}, u32[]{:S(2)}, u32[]{:S(2)}) async-start(bf16[128,6,2048]{2,1,0:T(8,128)(2,1)} %get-tuple-element.8), calls=%async_computation | async-start | bytes 8388608 | tf_op jit(solution)/shard_map/all_to_all | solution.py:62
  305.5 9.4 copy-start.3
  305.5 9.4 copy-start.8
  411.1 21.0 %all-to-all-start.3 = ((f32[128,1,6]{2,1,0:T(1,128)}), f32[128,1,6]{2,1,0:T(1,128)S(1)}, u32[]{:S(2)}, u32[]{:S(2)}) async-start(f32[128,1,6]{2,1,0:T(1,128)} %copy.37), calls=%async_computation.3 | async-start | bytes 131072 | tf_op jit(solution)/shard_map/all_to_all | solution.py:79
  419.8 5.6 copy-start.9
  419.8 5.6 copy-start.10
  419.8 5.6 copy-start.11
  432.0 14.5 %copy-start.5 = (s32[64,8]{0,1:T(8,128)S(1)}, s32[64,8]{0,1:T(8,128)}, u32[]{:S(2)}) copy-start(s32[64,8]{0,1:T(8,128)} %param.19) | copy-start | bytes 6148
  432.0 14.8 %copy-start.6 = (s32[64]{0:T(128)S(1)}, s32[64]{0:T(128)}, u32[]{:S(2)}) copy-start(s32[64]{0:T(128)} %param.21) | copy-start | bytes 772
  432.0 14.8 %copy-start.7 = (f32[64]{0:T(128)S(1)}, f32[64]{0:T(128)}, u32[]{:S(2)}) copy-start(f32[64]{0:T(128)} %param.18) | copy-start | bytes 772
  432.1 221.4 %copy-start.4 = (bf16[2048,128]{1,0:T(8,128)(2,1)S(1)}, bf16[2048,128]{1,0:T(8,128)(2,1)}, u32[]{:S(2)}) copy-start(bf16[2048,128]{1,0:T(8,128)(2,1)} %param.13) | copy-start | bytes 1572868
  432.1 479.4 %all-to-all-start.2 = ((bf16[128,6,2048]{2,1,0:T(8,128)(2,1)}), bf16[128,6,2048]{2,1,0:T(8,128)(2,1)}, u32[]{:S(2)}, u32[]{:S(2)}) async-start(bf16[128,6,2048]{2,1,0:T(8,128)(2,1)} %copy.35), calls=%async_computation.2 | async-start | bytes 8388608 | tf_op jit(solution)/shard_map/all_to_all | solution.py:78
  446.5 433.4 %all-reduce.3.cloned.1.call-start = ((), (), s32[]{:S(2)}) async-start(), calls=%async_computation.5 | async-start | bytes 2097152 | tf_op jit(solution)/shard_map/psum | solution.py:94
  659.8 250.4 %all-reduce.5.cloned.1.call-start = ((), (), s32[]{:S(2)}) async-start(), calls=%async_computation.6 | async-start | bytes 2097152 | tf_op jit(solution)/shard_map/psum | solution.py:95
  923.9 12.5 %copy-start.1 = (bf16[1,2048,768]{2,1,0:T(8,128)(2,1)S(1)}, bf16[1,2048,768]{2,1,0:T(8,128)(2,1)}, u32[]{:S(2)}) copy-start(bf16[1,2048,768]{2,1,0:T(8,128)(2,1)} %param.14) | copy-start | bytes 9437188
Sparse Core Ops, SparseCore 0:
  11.6 152.7 all-gather.1
  659.9 219.9 all-reduce.2
  882.5 27.6 all-reduce.4
